TPU v7x, 32 devices: a whole 2x2x4 slice. The times are simulated.
32 devices in a mesh: doc: 4 (over z), feat: 8 (over y, x, core).
Axes of the slice: x: 2, y: 2, z: 4, core: 2. Of those that a mesh axis runs over, the one named last changes fastest.
Arguments:
- documents: bfloat16 [512, 512], P('doc', 'feat'), may hold values from -6 to 6
- directions: bfloat16 [512, 32768], P('doc', 'feat'), may hold values from -0.5 to 0.5
- phase: float32 [32768], P('feat'), may hold values from -3.140625 to 3.140625
- amplitude: float32 [32768], P('feat'), may hold values from 0.4 to 2.3
- doc_weight: float32 [512], P('doc'), may hold values from 0.5 to 4.2
- labels: int32 [512], P('doc'), may hold values from 0 to 127
Outputs:
- margins: float32 [512, 128], P('doc')
- scaled_weights: float32 [32768, 128], P('feat')
All inputs are finite; a program needn't handle non-finite values.
Results may differ from a plain program's by a relative error of at most 0.0003.
Values may be sent and summed in bfloat16 or wider, within the bound.
A program may use at most 64 MiB of HBM per device.

v0:
```python
import jax
import jax.numpy as jnp
from jax import lax
from jax.sharding import PartitionSpec as P

C = 128
ITERS = 3
NEWTON = 3
HI = lax.Precision.HIGHEST
shrink_level = 0.1
ratio_floor = 1e-06


def logistic_prox(target, signs, weight_ratio):
    current = target
    for newton_step in range(NEWTON):
        chance = jax.nn.sigmoid(-signs * current)
        gradient = current - target - weight_ratio * signs * chance
        current = current - gradient / (1.0 + weight_ratio * chance * (1.0 - chance))
    return current


def shrink_values(target, limit):
    return target - jnp.clip(target, -limit, limit)


def per_device(documents, directions, phase, amplitude, doc_weight, labels):
    doc_count = documents.shape[0]
    width_tile = directions.shape[1]
    num_feat = lax.axis_size("feat")
    num_doc = lax.axis_size("doc")
    chunk = width_tile // num_doc
    row = lax.axis_index("doc")
    doc_rows = lax.all_gather(documents, "feat", axis=1, tiled=True)
    doc_full = lax.all_gather(doc_rows, "doc", axis=0, tiled=True)
    dir_chunk = lax.all_to_all(directions, "doc", split_axis=1, concat_axis=0, tiled=True)
    phase_c = lax.dynamic_slice_in_dim(phase, row * chunk, chunk, 0)
    amp_c = lax.dynamic_slice_in_dim(amplitude, row * chunk, chunk, 0)
    angles = jnp.dot(doc_full, dir_chunk, preferred_element_type=jnp.float32)
    features = jnp.sqrt(2.0 / width_tile) * amp_c * jnp.cos(angles + phase_c)
    blocks = features.reshape(num_doc, doc_count, chunk)
    gram = jnp.einsum("iac,ibc->iab", blocks, blocks, precision=HI)
    gram = lax.psum_scatter(gram, "doc", scatter_dimension=0, tiled=True)[0]
    eye = jnp.eye(doc_count, dtype=jnp.float32)
    factor = jnp.linalg.cholesky(eye + gram)
    lower_inv = lax.linalg.triangular_solve(factor, eye, left_side=True, lower=True)
    inverse = lax.dot_general(lower_inv, lower_inv, (((0,), (0,)), ((), ())), precision=HI)
    signs = jnp.where(labels[:, None] == jnp.arange(C, dtype=jnp.int32)[None, :], 1.0, -1.0).astype(
        jnp.float32
    )
    share_rows = doc_count // num_feat
    offset = lax.axis_index("feat") * share_rows
    signs = lax.dynamic_slice_in_dim(signs, offset, share_rows, 0)
    weight = lax.dynamic_slice_in_dim(doc_weight, offset, share_rows, 0)[:, None]
    rho = jnp.float32(1.0)
    margins = logistic_prox(jnp.zeros(signs.shape, jnp.float32), signs, weight / rho)
    sums = jnp.zeros(signs.shape, jnp.float32)
    duals_y = jnp.zeros(signs.shape, jnp.float32)
    part = jnp.zeros((doc_count, C), jnp.float32)
    image = jnp.zeros((doc_count, C), jnp.float32)
    weights = jnp.zeros((chunk, C), jnp.float32)
    product = jnp.zeros((doc_count, C), jnp.float32)
    for step in range(ITERS):
        correction = (margins - duals_y - sums) / num_feat
        correction = lax.all_gather(correction, "feat", axis=0, tiled=True)
        target = part + correction
        residue = target - image
        solved = jnp.dot(inverse, residue, precision=HI)
        applied = residue - solved
        part = target - solved
        sums = lax.psum_scatter(part, "feat", scatter_dimension=0, tiled=True)
        all_solved = lax.all_gather(solved, "doc", axis=0, tiled=True)
        lifted = lax.dot_general(features, all_solved, (((0,), (0,)), ((), ())), precision=HI)
        old_weights = weights
        old_margins = margins
        weights = shrink_values(weights + lifted / num_doc, shrink_level / (rho * num_doc))
        margins = logistic_prox(sums + duals_y, signs, weight / rho)
        duals_y = duals_y + sums - margins
        if step + 1 < ITERS:
            move = old_weights - weights
            if step == 0:
                d_move, d_solved, d_applied, d_lifted = (move, solved, applied, lifted)
            else:
                d_move = move - last_move / growth
                d_solved = solved - last_solved / growth
                d_applied = applied - last_applied / growth
                d_lifted = lifted - last_lifted / growth
            primal = (
                jnp.sum(num_doc * d_move * d_move + 2.0 * d_move * d_lifted)
                + jnp.sum(d_solved * d_applied)
                + jnp.sum((sums - margins) ** 2)
            )
            dual = num_doc * jnp.sum(move**2) + jnp.sum((margins - old_margins) ** 2)
            primal, dual = lax.psum((primal, dual), ("doc", "feat"))
            primal = jnp.maximum(primal, 0.0)
            new_product = jnp.dot(features, weights, precision=HI)
            new_product = lax.psum_scatter(new_product, "doc", scatter_dimension=0, tiled=True)
            growth = ((primal + ratio_floor) / (rho * rho * dual + ratio_floor)) ** 0.25
            rho = rho * growth
            duals_y = duals_y / growth
            image = new_product - (product - new_product + applied) / growth
            product = new_product
            last_move, last_solved, last_applied, last_lifted = (move, solved, applied, lifted)
    margins = lax.all_gather(margins, "feat", axis=0, tiled=True)
    weights = lax.all_gather(num_feat * weights, "doc", axis=0, tiled=True)
    return (margins, weights)


def solution(mesh):
    in_specs = (P("doc", "feat"), P("doc", "feat"), P("feat"), P("feat"), P("doc"), P("doc"))
    out_specs = (P("doc", None), P("feat", None))
    return jax.shard_map(
        per_device, mesh=mesh, in_specs=in_specs, out_specs=out_specs, check_vma=False
    )
```

profile of v0, /device:TPU:0, one launch (start us, length us, event | category | flops | bytes accessed | tf_op | source)
XLA Modules:
  0.0 383.9 jit_solution(2985545460666034803)
XLA Ops:
  7.2 2.3 copy.10
  9.4 6.3 %all-to-all-start = ((bf16[128,4,1024]{0,2,1:T(8,128)(2,1)}), bf16[128,4,1024]{0,2,1:T(8,128)(2,1)S(1)}, u32[]{:S(2)}, u32[]{:S(2)}) async-start(bf16[128,4,1024]{0,2,1:T(8,128)(2,1)} %bitcast), calls=%async_computation | async-start | bytes 2097152 | tf_op jit(solution)/shard_map/all_to_all | solution.py:36
  15.8 9.2 %all_gather.31 = bf16[128,512]{0,1:T(8,128)(2,1)S(1)} all-gather(bf16[128,64]{0,1:T(8,128)(2,1)S(1)} %copy-done.4), channel_id=1, replica_groups=mesh['doc'=4,'feat'=8] {'feat'}, dimensions={1}, use_global_device_ids=true | all-gather | bytes 147456 | tf_op jit(solution)/shard_map/all_gather | solution.py:34
  25.0 0.7 dynamic-slice_multiply_fusion
  25.7 25.3 %all_gather.32 = bf16[512,512]{0,1:T(8,128)(2,1)} all-gather(bf16[128,512]{0,1:T(8,128)(2,1)S(1)} %all_gather.31), channel_id=1, replica_groups=mesh['doc'=4,'feat'=8] {'doc'}, dimensions={0}, use_global_device_ids=true | all-gather | bytes 655360 | tf_op jit(solution)/shard_map/all_gather | solution.py:35
  51.0 0.5 copy.11
  51.6 8.3 %cosine_multiply_fusion = f32[512,1024]{1,0:T(8,128)S(1)} fusion(bf16[512,512]{0,1:T(8,128)(2,1)} %all_gather.32, bf16[512,1024]{1,0:T(8,128)(2,1)S(1)} %bitcast.38, f32[1024]{0:T(1024)S(1)} %dynamic-slice-done, f32[1024]{0:T(1024)S(1)} %dynamic-slice_multiply_fusion), kind=kOutput, calls=%fused_computation | convolution fusion | flops 537919488 | bytes 3678208 | tf_op jit(solution)/shard_map/dot_general | solution.py:39
  59.9 2.8 fusion.142
  62.7 0.0 reduce-scatter.7.cloned.1.call-update
  62.7 0.0 reduce-scatter.9.cloned.1.call-start
  62.8 0.1 dynamic-slice
  62.9 0.1 dynamic_slice.12
  62.9 0.1 broadcast_multiply_fusion
  63.1 9.4 %all_gather.30 = f32[128,128]{1,0:T(8,128)S(1)} all-gather(f32[16,128]{1,0:T(8,128)S(1)} %broadcast_multiply_fusion), channel_id=1, replica_groups=mesh['doc'=4,'feat'=8] {'feat'}, dimensions={0}, use_global_device_ids=true | all-gather | bytes 73728 | tf_op jit(solution)/shard_map/all_gather | solution.py:65
  72.5 14.2 %reduce-scatter.7.cloned.1.call-done = f32[1,128,128]{2,1,0:T(8,128)} async-done(((f32[4,128,128]{2,1,0:T(8,128)}), f32[1,128,128]{2,1,0:T(8,128)}) %reduce-scatter.7.cloned.1.call-update) | async-done | bytes 65552 | tf_op jit(solution)/shard_map/reduce_scatter | solution.py:43
  86.7 0.9 bitcast_add_fusion.1
  87.5 0.1 copy.12
  87.6 0.9 fusion.13
  88.5 11.7 %cholesky.18 = f32[128,128]{1,0:T(8,128)S(1)} custom-call(f32[128,128]{1,0:T(8,128)S(1)} %fusion.13), custom_call_target="Cholesky" | custom-call | tf_op jit(solution)/shard_map/jit(cholesky)/cholesky | solution.py:45
  100.2 0.6 compare_reduce_fusion
  100.9 0.7 fusion.10
  101.6 9.8 %custom-call.6 = f32[1,128,128]{1,2,0:T(8,128)S(1)} custom-call(f32[1,128,128]{2,1,0:T(8,128)S(1)} %fusion.10), custom_call_target="InvertDiagBlocksLowerTriangular" | custom-call | tf_op jit(solution)/shard_map/triangular_solve | solution.py:46
  111.4 0.3 fusion.11
  111.6 0.3 fusion.143
  111.9 1.5 multiply_reduce_fusion.3
  113.4 0.0 reduce-scatter.9.cloned.1.call-update
  113.5 0.0 reduce-scatter.11.cloned.1.call-start
  113.5 14.1 %all_gather.33 = f32[512,128]{1,0:T(8,128)S(1)} all-gather(f32[128,128]{1,0:T(8,128)S(1)} %get-tuple-element.23), channel_id=1, replica_groups=mesh['doc'=4,'feat'=8] {'doc'}, dimensions={0}, use_global_device_ids=true | all-gather | bytes 327680 | tf_op jit(solution)/shard_map/all_gather | solution.py:72
  127.6 4.1 %multiply_reduce_fusion.1 = (f32[]{:T(128)}, f32[]{:T(128)}, f32[1024,128]{1,0:T(8,128)S(1)}) fusion(f32[512,1024]{1,0:T(8,128)S(1)} %cosine_multiply_fusion, f32[512,128]{1,0:T(8,128)S(1)} %all_gather.33), kind=kOutput, calls=%fused_computation.13 | convolution fusion | flops 806879232 | bytes 2883592 | tf_op jit(solution)/shard_map/dot_general | solution.py:73
  131.7 2.5 fusion.6
  136.1 0.0 reduce-scatter.11.cloned.1.call-update
  136.1 0.0 reduce-scatter.13.cloned.1.call-start
  136.2 9.2 %reduce-scatter.9.cloned.1.call-done = f32[16,128]{1,0:T(8,128)} async-done(((f32[128,128]{1,0:T(8,128)}), f32[16,128]{1,0:T(8,128)}) %reduce-scatter.9.cloned.1.call-update) | async-done | bytes 8208 | tf_op jit(solution)/shard_map/reduce_scatter | solution.py:71
  145.4 1.5 multiply_reduce_fusion.6
  146.8 1.3 multiply_reduce_fusion.7
  149.3 39.3 %all-reduce.1 = (f32[]{:T(128)}, f32[]{:T(128)}) all-reduce(f32[]{:T(128)S(6)} %add.203, f32[]{:T(128)S(6)} %add.205), channel_id=1, replica_groups=mesh['doc'=4,'feat'=8] {'doc','feat'}, use_global_device_ids=true, to_apply=%region_7.8 | all-reduce | flops 2 | bytes 16 | tf_op jit(solution)/shard_map/psum | solution.py:94
  189.9 0.7 subtract_multiply_fusion.2
  190.6 10.2 %all_gather.34 = f32[128,128]{1,0:T(8,128)S(1)} all-gather(f32[16,128]{1,0:T(8,128)S(1)} %subtract_multiply_fusion.2), channel_id=1, replica_groups=mesh['doc'=4,'feat'=8] {'feat'}, dimensions={0}, use_global_device_ids=true | all-gather | bytes 73728 | tf_op jit(solution)/shard_map/all_gather | solution.py:65
  200.8 0.9 subtract_subtract_fusion
  201.7 1.5 multiply_reduce_fusion.2
  203.2 0.0 reduce-scatter.13.cloned.1.call-update
  203.2 0.0 reduce-scatter.15.cloned.1.call-start
  203.2 14.2 %all_gather.35 = f32[512,128]{1,0:T(8,128)S(1)} all-gather(f32[128,128]{1,0:T(8,128)S(1)} %get-tuple-element.25), channel_id=1, replica_groups=mesh['doc'=4,'feat'=8] {'doc'}, dimensions={0}, use_global_device_ids=true | all-gather | bytes 327680 | tf_op jit(solution)/shard_map/all_gather | solution.py:72
  217.4 4.2 %multiply_reduce_fusion = (f32[]{:T(128)}, f32[]{:T(128)}, f32[1024,128]{1,0:T(8,128)S(1)}) fusion(f32[1024,128]{1,0:T(8,128)S(1)} %get-tuple-element.24, f32[]{:T(128)S(6)} %neg.66, f32[]{:T(128)S(6)} %div.199, f32[]{:T(128)S(6)} %pow.6, f32[512,1024]{1,0:T(8,128)S(1)} %cosine_multiply_fusion, f32[512,128]{1,0:T(8,128)S(1)} %all_gather.35), kind=kOutput, calls=%fused_computation.11 | convolution fusion | flops 808189952 | bytes 3407892 | tf_op jit(solution)/shard_map/dot_general | solution.py:73
  221.6 2.5 fusion.137
  224.1 0.0 reduce-scatter.15.cloned.1.call-update
  224.2 0.0 reduce-scatter.17.cloned.1.call-start
  224.2 0.1 broadcast_divide_fusion.2
  226.1 9.7 %reduce-scatter.13.cloned.1.call-done = f32[16,128]{1,0:T(8,128)} async-done(((f32[128,128]{1,0:T(8,128)}), f32[16,128]{1,0:T(8,128)}) %reduce-scatter.13.cloned.1.call-update) | async-done | bytes 8208 | tf_op jit(solution)/shard_map/reduce_scatter | solution.py:71
  235.9 1.5 multiply_reduce_fusion.4
  238.5 39.4 %all-reduce = (f32[]{:T(128)}, f32[]{:T(128)}) all-reduce(f32[]{:T(128)S(6)} %add.219, f32[]{:T(128)S(6)} %add.221), channel_id=1, replica_groups=mesh['doc'=4,'feat'=8] {'doc','feat'}, use_global_device_ids=true, to_apply=%region_16.17 | all-reduce | flops 2 | bytes 16 | tf_op jit(solution)/shard_map/psum | solution.py:94
  279.2 0.7 subtract_multiply_fusion.1
  279.9 11.2 %all_gather.36 = f32[128,128]{1,0:T(8,128)} all-gather(f32[16,128]{1,0:T(8,128)S(1)} %subtract_multiply_fusion.1), channel_id=1, replica_groups=mesh['doc'=4,'feat'=8] {'feat'}, dimensions={0}, use_global_device_ids=true | all-gather | bytes 73728 | tf_op jit(solution)/shard_map/all_gather | solution.py:65
  291.1 1.8 fusion.140
  292.9 0.0 all-gather.2.cloned.1.call-start
  292.9 14.0 %all_gather.38 = f32[512,128]{1,0:T(8,128)S(1)} all-gather(f32[128,128]{1,0:T(8,128)S(1)} %get-tuple-element.28), channel_id=1, replica_groups=mesh['doc'=4,'feat'=8] {'doc'}, dimensions={0}, use_global_device_ids=true | all-gather | bytes 327680 | tf_op jit(solution)/shard_map/all_gather | solution.py:72
  306.9 4.2 %subtract_multiply_fusion = f32[1024,128]{1,0:T(8,128)} fusion(f32[512,1024]{1,0:T(8,128)S(1)} %cosine_multiply_fusion, f32[512,128]{1,0:T(8,128)S(1)} %all_gather.38, f32[]{:T(128)S(6)} %neg.70, f32[]{:T(128)S(6)} %div.220, f32[]{:T(128)S(6)} %neg.66, f32[]{:T(128)S(6)} %div.199, f32[1024,128]{1,0:T(8,128)S(1)} %get-tuple-element.26, ...), kind=kOutput, calls=%fused_computation.10 | convolution fusion | flops 807141376 | bytes 3932176 | tf_op jit(solution)/shard_map/dot_general | solution.py:73
  311.2 0.1 broadcast_divide_fusion.1
  311.2 14.3 %reduce-scatter.17.cloned.1.call-done = f32[16,128]{1,0:T(8,128)} async-done(((f32[128,128]{1,0:T(8,128)}), f32[16,128]{1,0:T(8,128)}) %reduce-scatter.17.cloned.1.call-update) | async-done | bytes 8208 | tf_op jit(solution)/shard_map/reduce_scatter | solution.py:71
  325.6 0.8 fusion.63
  326.4 9.2 %all_gather.37 = f32[128,128]{1,0:T(8,128)S(1)} all-gather(f32[16,128]{1,0:T(8,128)S(1)} %fusion.63), channel_id=1, replica_groups=mesh['doc'=4,'feat'=8] {'feat'}, dimensions={0}, use_global_device_ids=true | all-gather | bytes 73728 | tf_op jit(solution)/shard_map/all_gather | solution.py:104
  335.6 37.8 %all-gather.2.cloned.1.call-done = f32[4096,128]{1,0:T(8,128)} async-done(((f32[1024,128]{1,0:T(8,128)}), f32[4096,128]{1,0:T(8,128)}) %all-gather.2.cloned.1.call-update) | async-done | bytes 2097168 | tf_op jit(solution)/shard_map/all_gather | solution.py:105
  373.4 0.6 copy.15
  374.0 3.0 copy.16
  (29 shorter events, 0.1 us)
Async XLA Ops:
  7.2 8.6 %copy-start.4 = (bf16[128,64]{0,1:T(8,128)(2,1)S(1)}, bf16[128,64]{0,1:T(8,128)(2,1)}, u32[]{:S(2)}) copy-start(bf16[128,64]{0,1:T(8,128)(2,1)} %param.6) | copy-start | bytes 49156
  9.4 41.6 %all-to-all-start = ((bf16[128,4,1024]{0,2,1:T(8,128)(2,1)}), bf16[128,4,1024]{0,2,1:T(8,128)(2,1)S(1)}, u32[]{:S(2)}, u32[]{:S(2)}) async-start(bf16[128,4,1024]{0,2,1:T(8,128)(2,1)} %bitcast), calls=%async_computation | async-start | bytes 2097152 | tf_op jit(solution)/shard_map/all_to_all | solution.py:36
  15.8 70.9 %reduce-scatter.7.cloned.1.call-start = ((), (), s32[]{:S(2)}) async-start(), calls=%async_computation.7 | async-start | bytes 327680 | tf_op jit(solution)/shard_map/reduce_scatter | solution.py:43
  15.8 35.8 %dynamic-slice-start = ((f32[4096]{0:T(1024)}, s32[]{:T(128)}), f32[1024]{0:T(1024)S(1)}, s32[]{:S(2)}) async-start(f32[4096]{0:T(1024)} %param.8, s32[]{:T(128)} %select_n.18), calls=%async_computation.14 | async-start | bytes 8704 | tf_op jit(solution)/shard_map/dynamic_slice | solution.py:37
  59.9 2.9 copy-start.9
  59.9 2.9 copy-start.7
  62.7 82.6 %reduce-scatter.9.cloned.1.call-start = ((), (), s32[]{:S(2)}) async-start(), calls=%async_computation.8 | async-start | bytes 73728 | tf_op jit(solution)/shard_map/reduce_scatter | solution.py:71
  62.9 173.0 %copy-start.5 = (s32[16]{0:T(128)}, s32[16]{0:T(128)S(1)}, u32[]{:S(2)}) copy-start(s32[16]{0:T(128)S(1)} %dynamic-slice) | copy-start | bytes 196
  113.5 87.4 %reduce-scatter.11.cloned.1.call-start = ((), (), s32[]{:S(2)}) async-start(), calls=%async_computation.9 | async-start | bytes 327680 | tf_op jit(solution)/shard_map/reduce_scatter | solution.py:97
  131.7 69.2 %copy-start = (f32[128,128]{1,0:T(8,128)S(1)}, f32[128,128]{1,0:T(8,128)}, u32[]{:S(2)}) copy-start(f32[128,128]{1,0:T(8,128)} %get-tuple-element.20) | copy-start | bytes 196612
  136.1 99.8 %reduce-scatter.13.cloned.1.call-start = ((), (), s32[]{:S(2)}) async-start(), calls=%async_computation.10 | async-start | bytes 73728 | tf_op jit(solution)/shard_map/reduce_scatter | solution.py:71
  203.2 87.9 %reduce-scatter.15.cloned.1.call-start = ((), (), s32[]{:S(2)}) async-start(), calls=%async_computation.11 | async-start | bytes 327680 | tf_op jit(solution)/shard_map/reduce_scatter | solution.py:97
  221.6 69.5 %copy-start.1 = (f32[128,128]{1,0:T(8,128)S(1)}, f32[128,128]{1,0:T(8,128)}, u32[]{:S(2)}) copy-start(f32[128,128]{1,0:T(8,128)} %reduce-scatter.11.cloned.1.call-done) | copy-start | bytes 196612
  221.6 69.5 %copy-start.2 = (f32[128,128]{1,0:T(8,128)S(1)}, f32[128,128]{1,0:T(8,128)}, u32[]{:S(2)}) copy-start(f32[128,128]{1,0:T(8,128)} %get-tuple-element.22) | copy-start | bytes 196612
  224.2 101.4 %reduce-scatter.17.cloned.1.call-start = ((), (), s32[]{:S(2)}) async-start(), calls=%async_computation.12 | async-start | bytes 73728 | tf_op jit(solution)/shard_map/reduce_scatter | solution.py:71
  292.9 80.5 %all-gather.2.cloned.1.call-start = ((), (), s32[]{:S(2)}) async-start(), calls=%async_computation.13 | async-start | bytes 2621440 | tf_op jit(solution)/shard_map/all_gather | solution.py:105
  306.9 4.3 %copy-start.8 = (f32[128]{0:T(128)S(1)}, f32[128]{0:T(128)}, u32[]{:S(2)}) copy-start(f32[128]{0:T(128)} %param.10) | copy-start | bytes 1540
  306.9 18.7 %copy-start.3 = (f32[16,128]{1,0:T(8,128)S(1)}, f32[16,128]{1,0:T(8,128)}, u32[]{:S(2)}) copy-start(f32[16,128]{1,0:T(8,128)} %reduce-scatter.13.cloned.1.call-done) | copy-start | bytes 24580
  306.9 18.7 %copy-start.6 = (s32[16]{0:T(128)S(1)}, s32[16]{0:T(128)}, u32[]{:S(2)}) copy-start(s32[16]{0:T(128)} %copy-done.5) | copy-start | bytes 196
Sparse Core Ops, SparseCore 0:
  62.8 23.8 reduce-scatter.6
  113.6 31.7 reduce-scatter.8
  148.2 19.9 reduce-scatter.10
  203.3 32.4 reduce-scatter.12
  238.5 19.9 reduce-scatter.14
  293.0 32.5 reduce-scatter.16
  327.7 45.6 all-gather.1
where the time goes:
time: 385 us; the launch traced here: 384 us
  blocking collectives  195 us (51%)
  waiting for transfers between devices  85.3 us (22%)
  matrix products  33.9 us (9%)
  other arithmetic  32.9 us (9%)
  between operations  23 us (6%)
  local copies, waits for them, and re-layouts  6.75 us (2%)
  starting transfers between devices  6.6 us (2%)
    psum x2, blocking collectives, per_device(): primal, dual = lax.psum((primal, dual), ('doc', 'feat'))  78.7 us
    all_gather x3, blocking collectives, per_device(): all_solved = lax.all_gather(solved, 'doc', axis=0, tiled=True)  42.2 us
    all_gather x1, waiting for transfers between devices, per_device(): weights = lax.all_gather(num_feat * weights, 'doc', axis=0, tiled=True)  37.8 us
    reduce_scatter x3, waiting for transfers between devices, per_device(): sums = lax.psum_scatter(part, 'feat', scatter_dimension=0, tiled=True)  33.2 us
    all_gather x3, blocking collectives, per_device(): correction = lax.all_gather(correction, 'feat', axis=0, tiled=True)  30.8 us
    all_gather x1, blocking collectives, per_device(): doc_full = lax.all_gather(doc_rows, 'doc', axis=0, tiled=True)  25.3 us
    reduce_scatter x1, waiting for transfers between devices, per_device(): gram = lax.psum_scatter(gram, 'doc', scatter_dimension=0, tiled=True)[0]  14.2 us
    dot_general x3, matrix products, per_device(): lax.dot_general(features, all_solved, (((0,), (0,)), ((), ())), precision...  12.5 us
  transfers between devices with their start and end apart: 8, of which 5 were waited for; matrix products, arithmetic and copies ran while one was open for 7% of the time, Pallas kernels for 0%

commit v1 on v0

--- a/solution.py
+++ b/solution.py
@@ -91,7 +91,7 @@
                 + jnp.sum((sums - margins) ** 2)
             )
             dual = num_doc * jnp.sum(move**2) + jnp.sum((margins - old_margins) ** 2)
-            primal, dual = lax.psum((primal, dual), ("doc", "feat"))
+            primal, dual = lax.psum(lax.psum((primal, dual), "feat"), "doc")
             primal = jnp.maximum(primal, 0.0)
             new_product = jnp.dot(features, weights, precision=HI)
             new_product = lax.psum_scatter(new_product, "doc", scatter_dimension=0, tiled=True)

time: 385 us -> 351 us (0.912)
  blocking collectives: 195 us -> 166 us
  waiting for transfers between devices: 85.3 us -> 80.9 us
    psum x2 -> x4, blocking collectives: 78.7 us -> 50.1 us  [per_device(): primal, dual = lax.psum(lax.psum((primal, dual), 'feat'), 'doc')]
    reduce_scatter x3, waiting for transfers between devices: 33.2 us -> 28.8 us  [per_device(): sums = lax.psum_scatter(part, 'feat', scatter_dimension=0, tiled=True)]
where the time goes in v1:
time: 351 us; the launch traced here: 350 us
  blocking collectives  166 us (47%)
  waiting for transfers between devices  80.9 us (23%)
  matrix products  33.9 us (10%)
  other arithmetic  32.9 us (9%)
  between operations  23.2 us (7%)
  starting transfers between devices  6.86 us (2%)
  local copies, waits for them, and re-layouts  6.75 us (2%)
    psum x4, blocking collectives, per_device(): primal, dual = lax.psum(lax.psum((primal, dual), 'feat'), 'doc')  50.1 us
    all_gather x3, blocking collectives, per_device(): all_solved = lax.all_gather(solved, 'doc', axis=0, tiled=True)  42.9 us
    all_gather x1, waiting for transfers between devices, per_device(): weights = lax.all_gather(num_feat * weights, 'doc', axis=0, tiled=True)  37.8 us
    all_gather x3, blocking collectives, per_device(): correction = lax.all_gather(correction, 'feat', axis=0, tiled=True)  28.8 us
    reduce_scatter x3, waiting for transfers between devices, per_device(): sums = lax.psum_scatter(part, 'feat', scatter_dimension=0, tiled=True)  28.8 us
    all_gather x1, blocking collectives, per_device(): doc_full = lax.all_gather(doc_rows, 'doc', axis=0, tiled=True)  25.3 us
    reduce_scatter x1, waiting for transfers between devices, per_device(): gram = lax.psum_scatter(gram, 'doc', scatter_dimension=0, tiled=True)[0]  14.2 us
    dot_general x3, matrix products, per_device(): lax.dot_general(features, all_solved, (((0,), (0,)), ((), ())), precision...  12.5 us
  transfers between devices with their start and end apart: 8, of which 5 were waited for; matrix products, arithmetic and copies ran while one was open for 7% of the time, Pallas kernels for 0%

profile of v1, /device:TPU:0, one launch (start us, length us, event | category | flops | bytes accessed | tf_op | source)
XLA Modules:
  0.0 350.1 jit_solution(849150581545633026)
XLA Ops:
  7.2 2.3 copy.10
  9.4 6.3 %all-to-all-start = ((bf16[128,4,1024]{0,2,1:T(8,128)(2,1)}), bf16[128,4,1024]{0,2,1:T(8,128)(2,1)S(1)}, u32[]{:S(2)}, u32[]{:S(2)}) async-start(bf16[128,4,1024]{0,2,1:T(8,128)(2,1)} %bitcast), calls=%async_computation | async-start | bytes 2097152 | tf_op jit(solution)/shard_map/all_to_all | solution.py:36
  15.8 9.2 %all_gather.31 = bf16[128,512]{0,1:T(8,128)(2,1)S(1)} all-gather(bf16[128,64]{0,1:T(8,128)(2,1)S(1)} %copy-done.4), channel_id=1, replica_groups=mesh['doc'=4,'feat'=8] {'feat'}, dimensions={1}, use_global_device_ids=true | all-gather | bytes 147456 | tf_op jit(solution)/shard_map/all_gather | solution.py:34
  25.0 0.7 dynamic-slice_multiply_fusion
  25.7 25.3 %all_gather.32 = bf16[512,512]{0,1:T(8,128)(2,1)} all-gather(bf16[128,512]{0,1:T(8,128)(2,1)S(1)} %all_gather.31), channel_id=1, replica_groups=mesh['doc'=4,'feat'=8] {'doc'}, dimensions={0}, use_global_device_ids=true | all-gather | bytes 655360 | tf_op jit(solution)/shard_map/all_gather | solution.py:35
  51.0 0.5 copy.11
  51.6 8.3 %cosine_multiply_fusion = f32[512,1024]{1,0:T(8,128)S(1)} fusion(bf16[512,512]{0,1:T(8,128)(2,1)} %all_gather.32, bf16[512,1024]{1,0:T(8,128)(2,1)S(1)} %bitcast.38, f32[1024]{0:T(1024)S(1)} %dynamic-slice-done, f32[1024]{0:T(1024)S(1)} %dynamic-slice_multiply_fusion), kind=kOutput, calls=%fused_computation | convolution fusion | flops 537919488 | bytes 3678208 | tf_op jit(solution)/shard_map/dot_general | solution.py:39
  59.9 2.8 fusion.142
  62.7 0.0 reduce-scatter.7.cloned.1.call-update
  62.7 0.0 reduce-scatter.9.cloned.1.call-start
  62.8 0.1 dynamic-slice
  62.9 0.1 dynamic_slice.12
  62.9 0.1 broadcast_multiply_fusion
  63.1 9.4 %all_gather.30 = f32[128,128]{1,0:T(8,128)S(1)} all-gather(f32[16,128]{1,0:T(8,128)S(1)} %broadcast_multiply_fusion), channel_id=1, replica_groups=mesh['doc'=4,'feat'=8] {'feat'}, dimensions={0}, use_global_device_ids=true | all-gather | bytes 73728 | tf_op jit(solution)/shard_map/all_gather | solution.py:65
  72.5 14.2 %reduce-scatter.7.cloned.1.call-done = f32[1,128,128]{2,1,0:T(8,128)} async-done(((f32[4,128,128]{2,1,0:T(8,128)}), f32[1,128,128]{2,1,0:T(8,128)}) %reduce-scatter.7.cloned.1.call-update) | async-done | bytes 65552 | tf_op jit(solution)/shard_map/reduce_scatter | solution.py:43
  86.7 0.9 bitcast_add_fusion.1
  87.5 0.1 copy.12
  87.6 0.9 fusion.13
  88.5 11.7 %cholesky.18 = f32[128,128]{1,0:T(8,128)S(1)} custom-call(f32[128,128]{1,0:T(8,128)S(1)} %fusion.13), custom_call_target="Cholesky" | custom-call | tf_op jit(solution)/shard_map/jit(cholesky)/cholesky | solution.py:45
  100.2 0.6 compare_reduce_fusion
  100.9 0.7 fusion.10
  101.6 9.8 %custom-call.6 = f32[1,128,128]{1,2,0:T(8,128)S(1)} custom-call(f32[1,128,128]{2,1,0:T(8,128)S(1)} %fusion.10), custom_call_target="InvertDiagBlocksLowerTriangular" | custom-call | tf_op jit(solution)/shard_map/triangular_solve | solution.py:46
  111.4 0.3 fusion.11
  111.6 0.3 fusion.143
  111.9 1.5 multiply_reduce_fusion.3
  113.4 0.0 reduce-scatter.9.cloned.1.call-update
  113.5 0.0 reduce-scatter.11.cloned.1.call-start
  113.5 14.1 %all_gather.33 = f32[512,128]{1,0:T(8,128)S(1)} all-gather(f32[128,128]{1,0:T(8,128)S(1)} %get-tuple-element.27), channel_id=1, replica_groups=mesh['doc'=4,'feat'=8] {'doc'}, dimensions={0}, use_global_device_ids=true | all-gather | bytes 327680 | tf_op jit(solution)/shard_map/all_gather | solution.py:72
  127.6 4.1 %multiply_reduce_fusion.1 = (f32[]{:T(128)}, f32[]{:T(128)}, f32[1024,128]{1,0:T(8,128)S(1)}) fusion(f32[512,1024]{1,0:T(8,128)S(1)} %cosine_multiply_fusion, f32[512,128]{1,0:T(8,128)S(1)} %all_gather.33), kind=kOutput, calls=%fused_computation.13 | convolution fusion | flops 806879232 | bytes 2883592 | tf_op jit(solution)/shard_map/dot_general | solution.py:73
  131.7 2.5 fusion.6
  136.1 0.0 reduce-scatter.11.cloned.1.call-update
  136.1 0.0 reduce-scatter.13.cloned.1.call-start
  136.2 9.2 %reduce-scatter.9.cloned.1.call-done = f32[16,128]{1,0:T(8,128)} async-done(((f32[128,128]{1,0:T(8,128)}), f32[16,128]{1,0:T(8,128)}) %reduce-scatter.9.cloned.1.call-update) | async-done | bytes 8208 | tf_op jit(solution)/shard_map/reduce_scatter | solution.py:71
  145.4 1.5 multiply_reduce_fusion.6
  146.8 1.3 multiply_reduce_fusion.7
  149.3 13.1 %all-reduce.1 = (f32[]{:T(128)}, f32[]{:T(128)}) all-reduce(f32[]{:T(128)S(6)} %add.211, f32[]{:T(128)S(6)} %add.213), channel_id=1, replica_groups=mesh['doc'=4,'feat'=8] {'feat'}, use_global_device_ids=true, to_apply=%region_7.8 | all-reduce | flops 2 | bytes 16 | tf_op jit(solution)/shard_map/psum | solution.py:94
  162.4 12.0 %all-reduce.3 = (f32[]{:T(128)}, f32[]{:T(128)}) all-reduce(f32[]{:T(128)} %get-tuple-element.10, f32[]{:T(128)} %get-tuple-element.11), channel_id=1, replica_groups=mesh['doc'=4,'feat'=8] {'doc'}, use_global_device_ids=true, to_apply=%region_8.9 | all-reduce | flops 2 | bytes 16 | tf_op jit(solution)/shard_map/psum | solution.py:94
  175.7 0.7 subtract_multiply_fusion.2
  176.4 9.2 %all_gather.34 = f32[128,128]{1,0:T(8,128)S(1)} all-gather(f32[16,128]{1,0:T(8,128)S(1)} %subtract_multiply_fusion.2), channel_id=1, replica_groups=mesh['doc'=4,'feat'=8] {'feat'}, dimensions={0}, use_global_device_ids=true | all-gather | bytes 73728 | tf_op jit(solution)/shard_map/all_gather | solution.py:65
  185.6 0.9 subtract_subtract_fusion
  186.5 1.5 multiply_reduce_fusion.2
  188.0 0.0 reduce-scatter.15.cloned.1.call-start
  188.0 14.4 %all_gather.35 = f32[512,128]{1,0:T(8,128)S(1)} all-gather(f32[128,128]{1,0:T(8,128)S(1)} %get-tuple-element.29), channel_id=1, replica_groups=mesh['doc'=4,'feat'=8] {'doc'}, dimensions={0}, use_global_device_ids=true | all-gather | bytes 327680 | tf_op jit(solution)/shard_map/all_gather | solution.py:72
  202.4 4.2 %multiply_reduce_fusion = (f32[]{:T(128)}, f32[]{:T(128)}, f32[1024,128]{1,0:T(8,128)S(1)}) fusion(f32[1024,128]{1,0:T(8,128)S(1)} %get-tuple-element.28, f32[]{:T(128)S(6)} %neg.66, f32[]{:T(128)S(6)} %div.199, f32[]{:T(128)S(6)} %pow.6, f32[512,1024]{1,0:T(8,128)S(1)} %cosine_multiply_fusion, f32[512,128]{1,0:T(8,128)S(1)} %all_gather.35), kind=kOutput, calls=%fused_computation.11 | convolution fusion | flops 808189952 | bytes 3407892 | tf_op jit(solution)/shard_map/dot_general | solution.py:73
  206.6 2.5 fusion.137
  209.2 0.3 reduce-scatter.17.cloned.1.call-start
  209.5 0.1 broadcast_divide_fusion.2
  211.4 7.5 %reduce-scatter.13.cloned.1.call-done = f32[16,128]{1,0:T(8,128)} async-done(((f32[128,128]{1,0:T(8,128)}), f32[16,128]{1,0:T(8,128)}) %reduce-scatter.13.cloned.1.call-update) | async-done | bytes 8208 | tf_op jit(solution)/shard_map/reduce_scatter | solution.py:71
  218.9 1.5 multiply_reduce_fusion.4
  221.6 12.7 %all-reduce = (f32[]{:T(128)}, f32[]{:T(128)}) all-reduce(f32[]{:T(128)S(6)} %add.227, f32[]{:T(128)S(6)} %add.229), channel_id=1, replica_groups=mesh['doc'=4,'feat'=8] {'feat'}, use_global_device_ids=true, to_apply=%region_18.19 | all-reduce | flops 2 | bytes 16 | tf_op jit(solution)/shard_map/psum | solution.py:94
  234.3 12.4 %all-reduce.2 = (f32[]{:T(128)}, f32[]{:T(128)}) all-reduce(f32[]{:T(128)} %get-tuple-element.8, f32[]{:T(128)} %get-tuple-element.9), channel_id=1, replica_groups=mesh['doc'=4,'feat'=8] {'doc'}, use_global_device_ids=true, to_apply=%region_19.20 | all-reduce | flops 2 | bytes 16 | tf_op jit(solution)/shard_map/psum | solution.py:94
  248.1 0.7 subtract_multiply_fusion.1
  248.8 10.2 %all_gather.36 = f32[128,128]{1,0:T(8,128)} all-gather(f32[16,128]{1,0:T(8,128)S(1)} %subtract_multiply_fusion.1), channel_id=1, replica_groups=mesh['doc'=4,'feat'=8] {'feat'}, dimensions={0}, use_global_device_ids=true | all-gather | bytes 73728 | tf_op jit(solution)/shard_map/all_gather | solution.py:65
  259.0 1.8 fusion.140
  260.8 0.0 all-gather.2.cloned.1.call-start
  260.8 14.4 %all_gather.38 = f32[512,128]{1,0:T(8,128)S(1)} all-gather(f32[128,128]{1,0:T(8,128)S(1)} %get-tuple-element.32), channel_id=1, replica_groups=mesh['doc'=4,'feat'=8] {'doc'}, dimensions={0}, use_global_device_ids=true | all-gather | bytes 327680 | tf_op jit(solution)/shard_map/all_gather | solution.py:72
  275.2 4.2 %subtract_multiply_fusion = f32[1024,128]{1,0:T(8,128)} fusion(f32[512,1024]{1,0:T(8,128)S(1)} %cosine_multiply_fusion, f32[512,128]{1,0:T(8,128)S(1)} %all_gather.38, f32[]{:T(128)S(6)} %neg.70, f32[]{:T(128)S(6)} %div.220, f32[]{:T(128)S(6)} %neg.66, f32[]{:T(128)S(6)} %div.199, f32[1024,128]{1,0:T(8,128)S(1)} %get-tuple-element.30, ...), kind=kOutput, calls=%fused_computation.10 | convolution fusion | flops 807141376 | bytes 3932176 | tf_op jit(solution)/shard_map/dot_general | solution.py:73
  279.5 0.1 broadcast_divide_fusion.1
  279.6 12.1 %reduce-scatter.17.cloned.1.call-done = f32[16,128]{1,0:T(8,128)} async-done(((f32[128,128]{1,0:T(8,128)}), f32[16,128]{1,0:T(8,128)}) %reduce-scatter.17.cloned.1.call-update) | async-done | bytes 8208 | tf_op jit(solution)/shard_map/reduce_scatter | solution.py:71
  291.7 0.8 fusion.63
  292.6 9.2 %all_gather.37 = f32[128,128]{1,0:T(8,128)S(1)} all-gather(f32[16,128]{1,0:T(8,128)S(1)} %fusion.63), channel_id=1, replica_groups=mesh['doc'=4,'feat'=8] {'feat'}, dimensions={0}, use_global_device_ids=true | all-gather | bytes 73728 | tf_op jit(solution)/shard_map/all_gather | solution.py:104
  301.8 37.8 %all-gather.2.cloned.1.call-done = f32[4096,128]{1,0:T(8,128)} async-done(((f32[1024,128]{1,0:T(8,128)}), f32[4096,128]{1,0:T(8,128)}) %all-gather.2.cloned.1.call-update) | async-done | bytes 2097168 | tf_op jit(solution)/shard_map/all_gather | solution.py:105
  339.6 0.6 copy.15
  340.2 3.0 copy.16
  (31 shorter events, 0.2 us)
Async XLA Ops:
  7.2 8.6 %copy-start.4 = (bf16[128,64]{0,1:T(8,128)(2,1)S(1)}, bf16[128,64]{0,1:T(8,128)(2,1)}, u32[]{:S(2)}) copy-start(bf16[128,64]{0,1:T(8,128)(2,1)} %param.6) | copy-start | bytes 49156
  9.4 41.6 %all-to-all-start = ((bf16[128,4,1024]{0,2,1:T(8,128)(2,1)}), bf16[128,4,1024]{0,2,1:T(8,128)(2,1)S(1)}, u32[]{:S(2)}, u32[]{:S(2)}) async-start(bf16[128,4,1024]{0,2,1:T(8,128)(2,1)} %bitcast), calls=%async_computation | async-start | bytes 2097152 | tf_op jit(solution)/shard_map/all_to_all | solution.py:36
  15.8 70.9 %reduce-scatter.7.cloned.1.call-start = ((), (), s32[]{:S(2)}) async-start(), calls=%async_computation.7 | async-start | bytes 327680 | tf_op jit(solution)/shard_map/reduce_scatter | solution.py:43
  15.8 35.8 %dynamic-slice-start = ((f32[4096]{0:T(1024)}, s32[]{:T(128)}), f32[1024]{0:T(1024)S(1)}, s32[]{:S(2)}) async-start(f32[4096]{0:T(1024)} %param.8, s32[]{:T(128)} %select_n.18), calls=%async_computation.14 | async-start | bytes 8704 | tf_op jit(solution)/shard_map/dynamic_slice | solution.py:37
  59.9 2.9 copy-start.9
  59.9 2.9 copy-start.7
  62.7 82.6 %reduce-scatter.9.cloned.1.call-start = ((), (), s32[]{:S(2)}) async-start(), calls=%async_computation.8 | async-start | bytes 73728 | tf_op jit(solution)/shard_map/reduce_scatter | solution.py:71
  62.9 156.1 %copy-start.5 = (s32[16]{0:T(128)}, s32[16]{0:T(128)S(1)}, u32[]{:S(2)}) copy-start(s32[16]{0:T(128)S(1)} %dynamic-slice) | copy-start | bytes 196
  113.5 72.2 %reduce-scatter.11.cloned.1.call-start = ((), (), s32[]{:S(2)}) async-start(), calls=%async_computation.9 | async-start | bytes 327680 | tf_op jit(solution)/shard_map/reduce_scatter | solution.py:97
  131.7 54.0 %copy-start = (f32[128,128]{1,0:T(8,128)S(1)}, f32[128,128]{1,0:T(8,128)}, u32[]{:S(2)}) copy-start(f32[128,128]{1,0:T(8,128)} %get-tuple-element.24) | copy-start | bytes 196612
  136.1 82.8 %reduce-scatter.13.cloned.1.call-start = ((), (), s32[]{:S(2)}) async-start(), calls=%async_computation.10 | async-start | bytes 73728 | tf_op jit(solution)/shard_map/reduce_scatter | solution.py:71
  188.0 71.0 %reduce-scatter.15.cloned.1.call-start = ((), (), s32[]{:S(2)}) async-start(), calls=%async_computation.11 | async-start | bytes 327680 | tf_op jit(solution)/shard_map/reduce_scatter | solution.py:97
  206.6 52.4 %copy-start.1 = (f32[128,128]{1,0:T(8,128)S(1)}, f32[128,128]{1,0:T(8,128)}, u32[]{:S(2)}) copy-start(f32[128,128]{1,0:T(8,128)} %reduce-scatter.11.cloned.1.call-done) | copy-start | bytes 196612
  206.6 52.4 %copy-start.2 = (f32[128,128]{1,0:T(8,128)S(1)}, f32[128,128]{1,0:T(8,128)}, u32[]{:S(2)}) copy-start(f32[128,128]{1,0:T(8,128)} %get-tuple-element.26) | copy-start | bytes 196612
  209.2 82.5 %reduce-scatter.17.cloned.1.call-start = ((), (), s32[]{:S(2)}) async-start(), calls=%async_computation.12 | async-start | bytes 73728 | tf_op jit(solution)/shard_map/reduce_scatter | solution.py:71
  260.8 78.8 %all-gather.2.cloned.1.call-start = ((), (), s32[]{:S(2)}) async-start(), calls=%async_computation.13 | async-start | bytes 2621440 | tf_op jit(solution)/shard_map/all_gather | solution.py:105
  275.2 4.3 %copy-start.8 = (f32[128]{0:T(128)S(1)}, f32[128]{0:T(128)}, u32[]{:S(2)}) copy-start(f32[128]{0:T(128)} %param.10) | copy-start | bytes 1540
  275.2 16.5 %copy-start.3 = (f32[16,128]{1,0:T(8,128)S(1)}, f32[16,128]{1,0:T(8,128)}, u32[]{:S(2)}) copy-start(f32[16,128]{1,0:T(8,128)} %reduce-scatter.13.cloned.1.call-done) | copy-start | bytes 24580
  275.2 16.5 %copy-start.6 = (s32[16]{0:T(128)S(1)}, s32[16]{0:T(128)}, u32[]{:S(2)}) copy-start(s32[16]{0:T(128)} %copy-done.5) | copy-start | bytes 196
Sparse Core Ops, SparseCore 0:
  62.8 23.8 reduce-scatter.6
  113.6 31.7 reduce-scatter.8
  148.2 19.9 reduce-scatter.10
  188.1 30.7 reduce-scatter.12
  221.6 19.9 reduce-scatter.14
  260.9 30.7 reduce-scatter.16
  293.9 45.6 all-gather.1
